TPU v7x, 32 devices: a whole 2x2x4 slice. The times are simulated.
32 devices in a mesh: group: 2 (over y), seq: 4 (over z), head: 4 (over x, core).
Axes of the slice: x: 2, y: 2, z: 4, core: 2. Of those that a mesh axis runs over, the one named last changes fastest.
Arguments:
- tokens: bfloat16 [4096, 768], P(('group', 'seq')), parts along dimension 0, may hold values from -40 to 40
- w_qkv: bfloat16 [3, 768, 768], P(None, None, 'head'), may hold values from -1 to 1
- w_out: bfloat16 [768, 768], P('head'), may hold values from -0.75 to 0.75
- gain: float32 [768], P('head'), may hold values from 0.5 to 1.5
- bias: float32 [768], P('head'), may hold values from -3 to 3
- mid_offset: int32 [12], P('head'), may hold values from 0 to 7
- far_offset: int32 [12], P('head'), may hold values from 0 to 31
Outputs:
- encoded: bfloat16 [4096, 768], P(('group', 'seq'), 'head'), parts along dimension 0
There are 2 independent parts, one for each index of `group`. A program takes and returns all parts, laid end to end along the dimension named above; an argument that names none is the same for every part. Nothing has to cross between parts.
All inputs are finite; a program needn't handle non-finite values.
Results may differ from a plain program's by a relative error of at most 0.0085.
Values may be sent and summed in bfloat16 or wider, within the bound.
No kernel may reach another device: no remote copies, remote signals or barrier semaphores. Data moves between devices by JAX's collectives and lax.ppermute only.
A program may use at most 64 MiB of HBM per device.

v0:
```python
from functools import partial
import math
import jax
import jax.numpy as jnp
from jax import lax
from jax.sharding import PartitionSpec as P

HEADS = 12
SEG0 = 128
R1 = 8
R2 = 32
epsilon = 1e-05


def attend(queries, keys_in, values_in, scale):
    scores = (
        jnp.einsum("qhd,khd->hqk", queries, keys_in, preferred_element_type=jnp.float32) * scale
    )
    peaks = jnp.max(scores, axis=-1)
    shifted = jnp.exp(scores - peaks[..., None])
    masses = jnp.sum(shifted, axis=-1)
    weights = shifted.astype(jnp.bfloat16)
    summed = jnp.einsum("hqk,khd->qhd", weights, values_in, preferred_element_type=jnp.float32)
    result = summed / jnp.transpose(masses)[:, :, None]
    log_mass = jnp.transpose(peaks + jnp.log(masses))
    return (result, log_mass)


def pick(source, offset, rate):
    folded = source.reshape(source.shape[0] // rate, rate, source.shape[1], source.shape[2])
    chosen = lax.broadcasted_iota(jnp.int32, (rate, source.shape[1]), 0) == offset[None, :]
    kept = jnp.where(chosen[None, :, :, None], folded, jnp.zeros((), source.dtype))
    return jnp.sum(kept, axis=1)


def spread(result, log_mass, offset, rate):
    count = result.shape[0]
    chosen = lax.broadcasted_iota(jnp.int32, (rate, result.shape[1]), 0) == offset[None, :]
    full = jnp.where(chosen[None, :, :, None], result[:, None], 0.0)
    full = full.reshape(count * rate, result.shape[1], result.shape[2])
    mass_full = jnp.where(chosen[None], log_mass[:, None, :], -1e30).reshape(
        count * rate, result.shape[1]
    )
    return (full, mass_full)


def local(tokens, w_qkv, w_out, gain, bias, mid_offset, far_offset):
    rows_here = tokens.shape[0]
    width = tokens.shape[1]
    heads_here = mid_offset.shape[0]
    head_size = width // HEADS
    cols_here = heads_here * head_size
    scale = 1.0 / math.sqrt(head_size)
    projected = jnp.einsum("td,sde->ste", tokens, w_qkv, preferred_element_type=jnp.float32).astype(
        jnp.bfloat16
    )
    query = projected[0].reshape(rows_here, heads_here, head_size)
    keyed = projected[1].reshape(rows_here, heads_here, head_size)
    value = projected[2].reshape(rows_here, heads_here, head_size)
    blocks = rows_here // SEG0
    near_out, near_mass = jax.vmap(partial(attend, scale=scale))(
        query.reshape(blocks, SEG0, heads_here, head_size),
        keyed.reshape(blocks, SEG0, heads_here, head_size),
        value.reshape(blocks, SEG0, heads_here, head_size),
    )
    near_out = near_out.reshape(rows_here, heads_here, head_size)
    near_mass = near_mass.reshape(rows_here, heads_here)
    mid_count = rows_here // R1
    far_count = rows_here // R2
    mid_query = pick(query, mid_offset, R1)
    mid_stack = jnp.stack(
        [
            pick(keyed, mid_offset, R1).reshape(mid_count, cols_here),
            pick(value, mid_offset, R1).reshape(mid_count, cols_here),
        ]
    )
    far_query = pick(query, far_offset, R2)
    far_stack = jnp.stack(
        [
            pick(keyed, far_offset, R2).reshape(far_count, cols_here),
            pick(value, far_offset, R2).reshape(far_count, cols_here),
        ]
    )
    mid_devs = min(8, lax.axis_size("seq"))
    place = lax.axis_index("seq")
    gathered_mid, far_all = (
        lax.all_gather(mid_stack, "seq", axis=1, tiled=True),
        lax.all_gather(far_stack, "seq", axis=1, tiled=True),
    )
    first_row = place // mid_devs * (mid_devs * mid_count)
    mid_all = lax.dynamic_slice_in_dim(gathered_mid, first_row, mid_devs * mid_count, 1)
    mid_out, mid_mass = attend(
        mid_query,
        mid_all[0].reshape(-1, heads_here, head_size),
        mid_all[1].reshape(-1, heads_here, head_size),
        scale,
    )
    far_out, far_mass = attend(
        far_query,
        far_all[0].reshape(-1, heads_here, head_size),
        far_all[1].reshape(-1, heads_here, head_size),
        scale,
    )
    mid_full, mid_mfull = spread(mid_out, mid_mass, mid_offset, R1)
    far_full, far_mfull = spread(far_out, far_mass, far_offset, R2)
    top = jnp.maximum(jnp.maximum(near_mass, mid_mfull), far_mfull)
    near_weight = jnp.exp(near_mass - top)
    mid_weight = jnp.exp(mid_mfull - top)
    far_weight = jnp.exp(far_mfull - top)
    mixed = (
        near_weight[..., None] * near_out
        + mid_weight[..., None] * mid_full
        + far_weight[..., None] * far_full
    )
    mixed = mixed / (near_weight + mid_weight + far_weight)[..., None]
    attn = mixed.reshape(rows_here, cols_here).astype(jnp.bfloat16)
    head_count = lax.axis_size("head")
    head_place = lax.axis_index("head")
    piece_cols = width // head_count
    weight_cols = lax.all_to_all(w_out, "head", split_axis=1, concat_axis=0, tiled=True)
    summed = jnp.dot(
        lax.all_gather(attn, "head", axis=1, tiled=True),
        weight_cols,
        preferred_element_type=jnp.float32,
    )
    resid = (
        lax.dynamic_slice_in_dim(tokens, head_place * piece_cols, piece_cols, 1).astype(jnp.float32)
        + summed
    )
    totals, squares = lax.psum((jnp.sum(resid, axis=1), jnp.sum(resid * resid, axis=1)), "head")
    mean = totals / width
    var = squares / width - mean * mean
    normed_cols = (resid - mean[:, None]) * lax.rsqrt(var + epsilon)[:, None]
    return (normed_cols * gain + bias).astype(jnp.bfloat16)


def solution(mesh):
    in_specs = (
        P(("group", "seq"), None),
        P(None, None, "head"),
        P("head", None),
        P("head"),
        P("head"),
        P("head"),
        P("head"),
    )
    out_specs = P(("group", "seq"), "head")
    return jax.shard_map(local, mesh=mesh, in_specs=in_specs, out_specs=out_specs, check_vma=False)
```

profile of v0, /device:TPU:0, one launch (start us, length us, event | category | flops | bytes accessed | tf_op | source)
XLA Modules:
  0.0 76.6 jit_solution(17679054772339913622)
XLA Ops:
  0.0 2.0 %copy.128 = bf16[192,768]{0,1:T(8,128)(2,1)} copy(bf16[192,768]{1,0:T(8,128)(2,1)} %param.9) | data formatting | bytes 589824 | tf_op args[2]
  2.0 4.2 %all-to-all-start = ((bf16[192,4,192]{0,2,1:T(8,128)(2,1)}), bf16[192,4,192]{0,2,1:T(8,128)(2,1)}, u32[]{:S(2)}, u32[]{:S(2)}) async-start(bf16[192,4,192]{0,2,1:T(8,128)(2,1)} %bitcast.24), calls=%async_computation | async-start | bytes 786432 | tf_op jit(solution)/shard_map/all_to_all | solution.py:120
  6.2 0.7 fusion
  7.7 1.0 %reshape_reshape_squeeze.30 = bf16[64,8,3,64]{3,2,1,0:T(4,128)(2,1)} reshape(bf16[1,512,192]{2,1,0:T(8,128)(2,1)S(1)} %copy.104) | data formatting | bytes 393216 | tf_op jit(solution)/shard_map/reshape;reshape;squeeze | solution.py:30
  9.0 0.9 %reshape_reshape_squeeze.31 = bf16[64,8,3,64]{3,2,1,0:T(4,128)(2,1)} reshape(bf16[1,512,192]{2,1,0:T(8,128)(2,1)S(1)} %copy.106) | data formatting | bytes 393216 | tf_op jit(solution)/shard_map/reshape;reshape;squeeze | solution.py:30
  10.1 1.7 %reshape_reshape_squeeze.27 = bf16[4,128,3,64]{1,0,3,2:T(4,128)(2,1)} reshape(bf16[1,512,192]{1,2,0:T(8,128)(2,1)} %copy-done.4) | data formatting | bytes 393216 | tf_op jit(solution)/shard_map/reshape;reshape;squeeze | solution.py:62
  11.8 1.7 %reshape_reshape_squeeze.28 = bf16[4,128,3,64]{1,0,3,2:T(4,128)(2,1)} reshape(bf16[1,512,192]{1,2,0:T(8,128)(2,1)} %copy-done.3) | data formatting | bytes 393216 | tf_op jit(solution)/shard_map/reshape;reshape;squeeze | solution.py:63
  13.4 1.7 %reshape_reshape_squeeze.35 = bf16[4,128,3,64]{1,0,3,2:T(4,128)(2,1)} reshape(bf16[1,512,192]{1,2,0:T(8,128)(2,1)} %copy-done.2) | data formatting | bytes 393216 | tf_op jit(solution)/shard_map/reshape;reshape;squeeze | solution.py:64
  15.2 3.4 %select_reduce_fusion.5 = (bf16[64,3,64]{2,1,0:T(4,128)(2,1)}, bf16[64,3,64]{2,1,0:T(4,128)(2,1)}, bf16[64,3,64]{2,1,0:T(4,128)(2,1)}) fusion(bf16[64,8,3,64]{3,2,1,0:T(4,128)(2,1)S(1)} %reshape_reshape_squeeze.29, pred[8,3]{1,0:T(8,128)(4,1)S(1)} %iota_compare_fusion.1, bf16[64,8,3,64]{3,2,1,0:T(4,128)(2,1)S(1)} %copy-done.1, ...), kind=kLoop, calls=%fused_computation.21 | loop fusion | flops 552960 | bytes 663576 | tf_op jit(solution)/shard_map/reduce_sum | solution.py:33
  18.6 0.9 %copy.105 = bf16[64,3,64]{0,2,1:T(8,128)(2,1)S(1)} copy(bf16[64,3,64]{2,1,0:T(4,128)(2,1)} %get-tuple-element.11) | data formatting | bytes 49152 | tf_op jit(solution)/shard_map/reduce_sum | solution.py:33
  19.5 0.9 %copy.107 = bf16[64,3,64]{0,2,1:T(8,128)(2,1)S(1)} copy(bf16[64,3,64]{2,1,0:T(4,128)(2,1)} %get-tuple-element.12) | data formatting | bytes 49152 | tf_op jit(solution)/shard_map/reduce_sum | solution.py:33
  20.6 15.6 %all_gather.9 = bf16[2,256,192]{2,0,1:T(2,128)(2,1)S(1)} all-gather(bf16[2,64,192]{2,0,1:T(2,128)(2,1)S(1)} %copy.108), channel_id=1, replica_groups=mesh['group'=2,'seq'=4,'head'=4] {'seq'}, dimensions={1}, use_global_device_ids=true | all-gather | bytes 245760 | tf_op jit(solution)/shard_map/all_gather | solution.py:87
  36.2 0.4 fusion.31
  37.5 1.1 %select_reduce_fusion.2 = (bf16[16,3,64]{2,1,0:T(4,128)(2,1)S(1)}, bf16[16,3,64]{2,1,0:T(4,128)(2,1)S(1)}, bf16[16,3,64]{2,1,0:T(4,128)(2,1)S(1)}) fusion(bf16[16,32,3,64]{3,2,1,0:T(4,128)(2,1)S(1)} %reshape_reshape_squeeze.32, pred[32,3]{1,0:T(8,128)(4,1)S(1)} %iota_compare_fusion, bf16[16,32,3,64]{3,2,1,0:T(4,128)(2,1)S(1)} %reshape_reshape_squeeze.33, ...), kind=kLoop, calls=%fused_computation.18 | loop fusion | flops 580608 | bytes 608352 | tf_op jit(solution)/shard_map/reduce_sum | solution.py:33
  38.9 13.3 %all_gather.10 = bf16[2,64,192]{2,1,0:T(8,128)(2,1)S(1)} all-gather(bf16[2,16,192]{2,1,0:T(8,128)(2,1)S(1)} %pad_maximum_fusion.1), channel_id=1, replica_groups=mesh['group'=2,'seq'=4,'head'=4] {'seq'}, dimensions={1}, use_global_device_ids=true | all-gather | bytes 61440 | tf_op jit(solution)/shard_map/all_gather | solution.py:88
  53.8 0.6 broadcast_in_dim.184
  55.0 0.6 broadcast_in_dim.189
  56.5 0.5 copy-done.8
  57.5 1.1 %constant_dynamic-slice_fusion = bf16[512,192]{1,0:T(8,128)(2,1)S(1)} fusion(bf16[512,768]{1,0:T(8,128)(2,1)} %param.7, s32[]{:T(128)S(6)} %select_n.99), kind=kLoop, calls=%fused_computation.61 | loop fusion | bytes 393220 | tf_op jit(solution)/shard_map/dynamic_slice | solution.py:127
  59.0 8.8 %all_gather.11 = bf16[512,768]{0,1:T(8,128)(2,1)S(1)} all-gather(bf16[512,192]{0,1:T(8,128)(2,1)S(1)} %fusion.12), channel_id=1, replica_groups=mesh['group'=2,'seq'=4,'head'=4] {'head'}, dimensions={1}, use_global_device_ids=true | all-gather | bytes 983040 | tf_op jit(solution)/shard_map/all_gather | solution.py:122
  67.8 1.3 %copy.129 = bf16[4,192,192]{1,0,2:T(4,128)(2,1)S(1)} copy(bf16[4,192,192]{1,2,0:T(8,128)(2,1)} %bitcast.25) | data formatting | bytes 589824 | tf_op jit(solution)/shard_map/all_to_all | solution.py:120
  69.4 0.3 fusion.28
  69.8 6.0 %all-reduce = (f32[512]{0:T(512)S(1)}, f32[512]{0:T(512)S(1)}) all-reduce(f32[512]{0:T(512)S(1)} %get-tuple-element.6, f32[512]{0:T(512)S(1)} %get-tuple-element.5), channel_id=1, replica_groups=mesh['group'=2,'seq'=4,'head'=4] {'head'}, use_global_device_ids=true, to_apply=%region_15.16 | all-reduce | flops 1024 | bytes 8192 | tf_op jit(solution)/shard_map/psum | solution.py:130
  75.8 0.8 %add_convert_fusion = bf16[512,192]{0,1:T(8,128)(2,1)} fusion(f32[512,192]{0,1:T(8,128)S(1)} %get-tuple-element.34, f32[192]{0:T(256)S(1)} %copy-done.10, f32[192]{0:T(256)S(1)} %copy-done.11, f32[512]{0:T(512)S(1)} %get-tuple-element.27, f32[512]{0:T(512)S(1)} %get-tuple-element.26), kind=kLoop, calls=%fused_computation.28 | loop fusion | flops 491520 | bytes 595456 | tf_op jit(solution)/shard_map/convert_element_type | solution.py:134
  (81 shorter events, 6.8 us)
Async XLA Ops:
  0.0 6.2 %copy-start = (bf16[3,768,192]{1,2,0:T(8,128)(2,1)S(1)}, bf16[3,768,192]{1,2,0:T(8,128)(2,1)}, u32[]{:S(2)}) copy-start(bf16[3,768,192]{1,2,0:T(8,128)(2,1)} %param.8) | copy-start | bytes 2654212
  0.0 6.2 %copy-start.9 = (bf16[512,768]{1,0:T(8,128)(2,1)S(1)}, bf16[512,768]{1,0:T(8,128)(2,1)}, u32[]{:S(2)}) copy-start(bf16[512,768]{1,0:T(8,128)(2,1)} %param.7) | copy-start | bytes 2359300
  2.0 65.7 %all-to-all-start = ((bf16[192,4,192]{0,2,1:T(8,128)(2,1)}), bf16[192,4,192]{0,2,1:T(8,128)(2,1)}, u32[]{:S(2)}, u32[]{:S(2)}) async-start(bf16[192,4,192]{0,2,1:T(8,128)(2,1)} %bitcast.24), calls=%async_computation | async-start | bytes 786432 | tf_op jit(solution)/shard_map/all_to_all | solution.py:120
  6.9 0.7 copy-start.3
  7.0 0.7 copy-start.4
  7.0 1.8 %copy-start.2 = (bf16[1,512,192]{1,2,0:T(8,128)(2,1)}, bf16[1,512,192]{1,2,0:T(8,128)(2,1)S(1)}, u32[]{:S(2)}) copy-start(bf16[1,512,192]{1,2,0:T(8,128)(2,1)S(1)} %get-tuple-element.19) | copy-start | bytes 589828
  9.9 5.2 %copy-start.13 = (s32[3]{0:T(128)S(1)}, s32[3]{0:T(128)}, u32[]{:S(2)}) copy-start(s32[3]{0:T(128)} %param.12) | copy-start | bytes 40
  10.0 5.1 %copy-start.1 = (bf16[64,8,3,64]{3,2,1,0:T(4,128)(2,1)S(1)}, bf16[64,8,3,64]{3,2,1,0:T(4,128)(2,1)}, u32[]{:S(2)}) copy-start(bf16[64,8,3,64]{3,2,1,0:T(4,128)(2,1)} %reshape_reshape_squeeze.30) | copy-start | bytes 589828
  20.5 16.3 %copy-start.7 = (bf16[64,3,64]{2,1,0:T(4,128)(2,1)S(1)}, bf16[64,3,64]{2,1,0:T(4,128)(2,1)}, u32[]{:S(2)}) copy-start(bf16[64,3,64]{2,1,0:T(4,128)(2,1)} %get-tuple-element.10) | copy-start | bytes 73732
  36.2 1.2 %copy-start.12 = (s32[3]{0:T(128)S(1)}, s32[3]{0:T(128)}, u32[]{:S(2)}) copy-start(s32[3]{0:T(128)} %param.13) | copy-start | bytes 40
  55.0 0.9 %copy-start.5 = (bf16[4,128,3,64]{1,0,3,2:T(4,128)(2,1)S(1)}, bf16[4,128,3,64]{1,0,3,2:T(4,128)(2,1)}, u32[]{:S(2)}) copy-start(bf16[4,128,3,64]{1,0,3,2:T(4,128)(2,1)} %reshape_reshape_squeeze.27) | copy-start | bytes 589828
  55.0 1.0 %copy-start.6 = (bf16[4,128,3,64]{1,0,3,2:T(4,128)(2,1)S(1)}, bf16[4,128,3,64]{1,0,3,2:T(4,128)(2,1)}, u32[]{:S(2)}) copy-start(bf16[4,128,3,64]{1,0,3,2:T(4,128)(2,1)} %reshape_reshape_squeeze.28) | copy-start | bytes 589828
  56.0 0.9 %copy-start.8 = (bf16[4,128,3,64]{1,0,3,2:T(4,128)(2,1)S(1)}, bf16[4,128,3,64]{1,0,3,2:T(4,128)(2,1)}, u32[]{:S(2)}) copy-start(bf16[4,128,3,64]{1,0,3,2:T(4,128)(2,1)} %reshape_reshape_squeeze.35) | copy-start | bytes 589828
  69.1 6.7 %copy-start.10 = (f32[192]{0:T(256)S(1)}, f32[192]{0:T(256)}, u32[]{:S(2)}) copy-start(f32[192]{0:T(256)} %param.11) | copy-start | bytes 2308
  69.1 6.7 %copy-start.11 = (f32[192]{0:T(256)S(1)}, f32[192]{0:T(256)}, u32[]{:S(2)}) copy-start(f32[192]{0:T(256)} %param.10) | copy-start | bytes 2308
where the time goes:
time: 77.2 us; the launch traced here: 76.6 us
  blocking collectives  43.7 us (57%)
  local copies, waits for them, and re-layouts  19.7 us (26%)
  other arithmetic  6.08 us (8%)
  starting transfers between devices  4.21 us (5%)
  matrix products  2.49 us (3%)
    all_gather x1, blocking collectives, local(): lax.all_gather(mid_stack, 'seq', axis=1, tiled=True)  15.6 us
    all_gather x1, blocking collectives, local(): lax.all_gather(far_stack, 'seq', axis=1, tiled=True)  13.3 us
    all_gather x1, blocking collectives, local(): lax.all_gather(attn, 'head', axis=1, tiled=True)  8.79 us
    psum x1, blocking collectives, local(): lax.psum((jnp.sum(resid, axis=1), jnp.sum(resid * resid, axis=1)), 'head')  6.01 us
    reduce_sum x2, other arithmetic, pick(): return jnp.sum(kept, axis=1)  4.51 us
    all_to_all x1, starting transfers between devices, local(): lax.all_to_all(w_out, 'head', split_axis=1, concat_axis=0, tiled=True)  4.21 us
    unnamed x30, local copies, waits for them, and re-layouts  3.03 us
    another operation x6, local copies, waits for them, and re-layouts, pick(): source.reshape(source.shape[0] // rate, rate, source.shape[1], source.sha...  2.48 us
  transfers between devices with their start and end apart: 1, of which 0 were waited for; matrix products, arithmetic and copies ran while one was open for 29% of the time, Pallas kernels for 0%

commit v1 on v0

--- a/solution.py
+++ b/solution.py
@@ -10,6 +10,27 @@
 R1 = 8
 R2 = 32
 epsilon = 1e-05
+
+
+def laid_out(pieces, dim):
+    pieces = jnp.moveaxis(pieces, 0, dim)
+    dims = pieces.shape
+    return pieces.reshape(*dims[:dim], dims[dim] * dims[dim + 1], *dims[dim + 2 :])
+
+
+def collected_by_bits(shard, axis):
+    count, index = (lax.axis_size(axis), lax.axis_index(axis))
+    parts, bit = (shard[None], 1)
+    while bit < count:
+        other = lax.ppermute(parts, axis, [(i, i ^ bit) for i in range(count)])
+        low = index & bit == 0
+        parts = jnp.concatenate([jnp.where(low, parts, other), jnp.where(low, other, parts)])
+        bit *= 2
+    return parts
+
+
+def gather_by_bits(array, axis, dim):
+    return laid_out(collected_by_bits(array, axis), dim)
 
 
 def attend(queries, keys_in, values_in, scale):
@@ -84,7 +105,7 @@
     mid_devs = min(8, lax.axis_size("seq"))
     place = lax.axis_index("seq")
     gathered_mid, far_all = (
-        lax.all_gather(mid_stack, "seq", axis=1, tiled=True),
+        gather_by_bits(mid_stack, "seq", 1),
         lax.all_gather(far_stack, "seq", axis=1, tiled=True),
     )
     first_row = place // mid_devs * (mid_devs * mid_count)

time: 77.2 us -> 67.5 us (0.87)
  blocking collectives: 43.7 us -> 28.4 us
  waiting for transfers between devices: 0.01 us -> 5.3 us
  local copies, waits for them, and re-layouts: 19.7 us -> 14.6 us
  starting transfers between devices: 4.21 us -> 7.84 us
  matrix products: 2.49 us -> 4.38 us
    all_gather x1 -> x0, blocking collectives: 15.6 us -> none  [local(): lax.all_gather(mid_stack, 'seq', axis=1, tiled=True)]
    ppermute x0 -> x2, waiting for transfers between devices: none -> 5.3 us  [collected_by_bits(): other = lax.ppermute(parts, axis, [(i, i ^ bit) for i in range(count)])]
    ppermute x0 -> x2, starting transfers between devices: none -> 3.74 us  [collected_by_bits(): other = lax.ppermute(parts, axis, [(i, i ^ bit) for i in range(count)])]
    unnamed x30 -> x24, local copies, waits for them, and re-layouts: 3.03 us -> 5.14 us
    another operation x1, local copies, waits for them, and re-layouts: 1.71 us -> 0.05 us  [local(): query.reshape(blocks, SEG0, heads_here, head_size)]
    another operation x1, local copies, waits for them, and re-layouts: 1.66 us -> 0.05 us  [local(): keyed.reshape(blocks, SEG0, heads_here, head_size)]
    another operation x6, local copies, waits for them, and re-layouts: 2.48 us -> 0.87 us  [pick(): source.reshape(source.shape[0] // rate, rate, source.shape[1], source.sha...]
    another operation x1, local copies, waits for them, and re-layouts: 1.65 us -> 0.05 us  [local(): value.reshape(blocks, SEG0, heads_here, head_size)]
  transfers between devices with their start and end apart: 1 -> 3, of which waited for: 0 -> 1; matrix products, arithmetic and copies ran while one was open for 29% -> 19% of each run, Pallas kernels for 0% -> 0%
where the time goes in v1:
time: 67.5 us; the launch traced here: 66.9 us
  blocking collectives  28.4 us (42%)
  local copies, waits for them, and re-layouts  14.6 us (22%)
  starting transfers between devices  7.84 us (12%)
  other arithmetic  5.91 us (9%)
  waiting for transfers between devices  5.3 us (8%)
  matrix products  4.38 us (6%)
    all_gather x1, blocking collectives, local(): lax.all_gather(far_stack, 'seq', axis=1, tiled=True)  13.3 us
    all_gather x1, blocking collectives, local(): lax.all_gather(attn, 'head', axis=1, tiled=True)  9.07 us
    psum x1, blocking collectives, local(): lax.psum((jnp.sum(resid, axis=1), jnp.sum(resid * resid, axis=1)), 'head')  6.01 us
    ppermute x2, waiting for transfers between devices, collected_by_bits(): other = lax.ppermute(parts, axis, [(i, i ^ bit) for i in range(count)])  5.3 us
    unnamed x24, local copies, waits for them, and re-layouts  5.14 us
    all_to_all x1, starting transfers between devices, local(): lax.all_to_all(w_out, 'head', split_axis=1, concat_axis=0, tiled=True)  4.1 us
    ppermute x2, starting transfers between devices, collected_by_bits(): other = lax.ppermute(parts, axis, [(i, i ^ bit) for i in range(count)])  3.74 us
    reduce_sum x2, other arithmetic, pick(): return jnp.sum(kept, axis=1)  3.37 us
  transfers between devices with their start and end apart: 3, of which 1 were waited for; matrix products, arithmetic and copies ran while one was open for 19% of the time, Pallas kernels for 0%

profile of v1, /device:TPU:0, one launch (start us, length us, event | category | flops | bytes accessed | tf_op | source)
XLA Modules:
  0.0 66.9 jit_solution(11906557180900426708)
XLA Ops:
  0.0 1.2 %copy-done = bf16[3,768,192]{1,2,0:T(8,128)(2,1)S(1)} copy-done((bf16[3,768,192]{1,2,0:T(8,128)(2,1)S(1)}, bf16[3,768,192]{1,2,0:T(8,128)(2,1)}, u32[]{:S(2)}) %copy-start) | copy-done | bytes 884760
  1.2 1.8 %fusion = bf16[3,512,192]{1,2,0:T(8,128)(2,1)S(1)} fusion(bf16[3,768,192]{1,2,0:T(8,128)(2,1)S(1)} %copy-done, bf16[512,768]{1,0:T(8,128)(2,1)} %param.7), kind=kOutput, calls=%fused_computation.2 | convolution fusion | flops 453279744 | bytes 2260992 | tf_op jit(solution)/shard_map/td,sde->ste/dot_general | solution.py:75
  3.3 0.4 copy-done.3
  4.5 2.3 %select_reduce_fusion.5 = (bf16[64,3,64]{2,1,0:T(4,128)(2,1)}, bf16[64,3,64]{2,1,0:T(4,128)(2,1)}, bf16[64,3,64]{2,1,0:T(4,128)(2,1)S(1)}) fusion(bf16[64,8,3,64]{3,2,1,0:T(4,128)(2,1)S(1)} %reshape_reshape_squeeze.29, pred[8,3]{1,0:T(8,128)(4,1)S(1)} %iota_compare_fusion.1, bf16[64,8,3,64]{3,2,1,0:T(4,128)(2,1)S(1)} %reshape_reshape_squeeze.30, ...), kind=kLoop, calls=%fused_computation.21 | loop fusion | flops 552960 | bytes 663576 | tf_op jit(solution)/shard_map/reduce_sum | solution.py:54
  6.7 0.9 %copy.80 = bf16[64,3,64]{0,2,1:T(8,128)(2,1)S(1)} copy(bf16[64,3,64]{2,1,0:T(4,128)(2,1)} %get-tuple-element.11) | data formatting | bytes 49152 | tf_op jit(solution)/shard_map/reduce_sum | solution.py:54
  7.9 3.1 %collective-permute-start = (bf16[1,2,64,192]{3,2,1,0:T(8,128)(2,1)S(1)}, bf16[1,2,64,192]{3,2,1,0:T(8,128)(2,1)}, u32[]{:S(2)}, u32[]{:S(2)}) collective-permute-start(bf16[1,2,64,192]{3,2,1,0:T(8,128)(2,1)S(1)} %bitcast.121), channel_id=1, source_target_pairs={{0,4},{4,0},{8,12},{12,8},{1,5},{5,1},{9,13},{13,9},{2,6},{6,2},{1... | collective-permute-start | bytes 147464 | tf_op jit(solution)/shard_map/ppermute | solution.py:25
  11.0 1.9 %copy.103 = bf16[192,768]{0,1:T(8,128)(2,1)} copy(bf16[192,768]{1,0:T(8,128)(2,1)} %param.9) | data formatting | bytes 589824 | tf_op args[2]
  12.9 4.1 %all-to-all-start = ((bf16[192,4,192]{0,2,1:T(8,128)(2,1)}), bf16[192,4,192]{0,2,1:T(8,128)(2,1)}, u32[]{:S(2)}, u32[]{:S(2)}) async-start(bf16[192,4,192]{0,2,1:T(8,128)(2,1)} %bitcast.24), calls=%async_computation | async-start | bytes 786432 | tf_op jit(solution)/shard_map/all_to_all | solution.py:141
  17.5 0.4 copy-done.4
  18.3 1.1 %select_reduce_fusion.2 = (bf16[16,3,64]{2,1,0:T(4,128)(2,1)S(1)}, bf16[16,3,64]{2,1,0:T(4,128)(2,1)S(1)}, bf16[16,3,64]{2,1,0:T(4,128)(2,1)S(1)}) fusion(bf16[16,32,3,64]{3,2,1,0:T(4,128)(2,1)S(1)} %reshape_reshape_squeeze.32, pred[32,3]{1,0:T(8,128)(4,1)S(1)} %iota_compare_fusion, bf16[16,32,3,64]{3,2,1,0:T(4,128)(2,1)S(1)} %reshape_reshape_squeeze.33, ...), kind=kLoop, calls=%fused_computation.18 | loop fusion | flops 580608 | bytes 608352 | tf_op jit(solution)/shard_map/reduce_sum | solution.py:54
  19.6 13.3 %all_gather.6 = bf16[2,64,192]{2,1,0:T(8,128)(2,1)S(1)} all-gather(bf16[2,16,192]{2,1,0:T(8,128)(2,1)S(1)} %pad_maximum_fusion.2), channel_id=1, replica_groups=mesh['group'=2,'seq'=4,'head'=4] {'seq'}, dimensions={1}, use_global_device_ids=true | all-gather | bytes 61440 | tf_op jit(solution)/shard_map/all_gather | solution.py:109
  34.2 1.0 %fusion.1 = f32[4,128,3,64]{1,3,2,0:T(8,128)} fusion(f32[4,3,128,128]{2,3,1,0:T(8,128)S(1)} %get-tuple-element.37, f32[4,3,128]{2,1,0:T(4,128)S(1)} %get-tuple-element.36, bf16[4,128,3,64]{1,0,3,2:T(4,128)(2,1)S(1)} %reshape_reshape_squeeze.35, f32[4,128,3]{1,2,0:T(4,128)S(1)} %bitcast.126), kind=kOutput, calls=%fused_computation.4 | convolution fusion | flops 25657344 | bytes 1388544 | tf_op jit(solution)/shard_map/vmap(hqk,khd->qhd)/dot_general | solution.py:44
  36.0 0.6 broadcast_in_dim.193
  36.8 0.8 %copy-done.5 = f32[4,128,3,64]{1,3,2,0:T(8,128)S(1)} copy-done((f32[4,128,3,64]{1,3,2,0:T(8,128)S(1)}, f32[4,128,3,64]{1,3,2,0:T(8,128)}, u32[]{:S(2)}) %copy-start.5) | copy-done | bytes 393240
  37.8 0.9 %broadcast_select_fusion.3 = (bf16[1,2,64,192]{3,2,1,0:T(8,128)(2,1)S(1)}, bf16[1,2,64,192]{3,2,1,0:T(8,128)(2,1)S(1)}) fusion(bf16[1,2,64,192]{3,2,1,0:T(8,128)(2,1)} %collective-permute-done, pred[]{:T(512)S(6)} %eq.31, bf16[2,64,192]{2,1,0:T(8,128)(2,1)S(1)} %copy.83), kind=kLoop, calls=%fused_computation.45 | loop fusion | flops 49152 | bytes 196609 | tf_op jit(solution)/shard_map/jit(_where)/select_n | solution.py:27
  38.7 0.7 collective-permute-start.1
  39.4 1.1 %constant_dynamic-slice_fusion = bf16[512,192]{1,0:T(8,128)(2,1)S(1)} fusion(bf16[512,768]{1,0:T(8,128)(2,1)} %param.7, s32[]{:T(128)S(6)} %select_n.123), kind=kLoop, calls=%fused_computation.67 | loop fusion | bytes 393220 | tf_op jit(solution)/shard_map/dynamic_slice | solution.py:148
  40.7 5.3 %collective-permute-done.1 = bf16[2,2,64,192]{3,2,1,0:T(8,128)(2,1)S(1)} collective-permute-done((bf16[2,2,64,192]{3,2,1,0:T(8,128)(2,1)S(1)}, bf16[2,2,64,192]{3,2,1,0:T(8,128)(2,1)S(1)}, u32[]{:S(2)}, u32[]{:S(2)}) %collective-permute-start.1) | collective-permute-done | bytes 98336 | tf_op jit(solution)/shard_map/ppermute | solution.py:25
  48.0 0.6 broadcast_in_dim.188
  48.9 9.1 %all_gather.7 = bf16[512,768]{0,1:T(8,128)(2,1)S(1)} all-gather(bf16[512,192]{0,1:T(8,128)(2,1)S(1)} %fusion.12), channel_id=1, replica_groups=mesh['group'=2,'seq'=4,'head'=4] {'head'}, dimensions={1}, use_global_device_ids=true | all-gather | bytes 983040 | tf_op jit(solution)/shard_map/all_gather | solution.py:143
  58.0 1.3 %copy.104 = bf16[4,192,192]{1,0,2:T(4,128)(2,1)S(1)} copy(bf16[4,192,192]{1,2,0:T(8,128)(2,1)} %bitcast.25) | data formatting | bytes 589824 | tf_op jit(solution)/shard_map/all_to_all | solution.py:141
  59.7 0.4 fusion.28
  60.0 6.0 %all-reduce = (f32[512]{0:T(512)S(1)}, f32[512]{0:T(512)S(1)}) all-reduce(f32[512]{0:T(512)S(1)} %get-tuple-element.6, f32[512]{0:T(512)S(1)} %get-tuple-element.5), channel_id=1, replica_groups=mesh['group'=2,'seq'=4,'head'=4] {'head'}, use_global_device_ids=true, to_apply=%region_15.16 | all-reduce | flops 1024 | bytes 8192 | tf_op jit(solution)/shard_map/psum | solution.py:151
  66.1 0.8 %add_convert_fusion = bf16[512,192]{0,1:T(8,128)(2,1)} fusion(f32[512,192]{0,1:T(8,128)S(1)} %get-tuple-element.38, f32[192]{0:T(256)S(1)} %copy-done.7, f32[192]{0:T(256)S(1)} %copy-done.8, f32[512]{0:T(512)S(1)} %get-tuple-element.31, f32[512]{0:T(512)S(1)} %get-tuple-element.30), kind=kLoop, calls=%fused_computation.28 | loop fusion | flops 491520 | bytes 595456 | tf_op jit(solution)/shard_map/convert_element_type | solution.py:155
  (84 shorter events, 7.5 us)
Async XLA Ops:
  0.0 1.2 %copy-start = (bf16[3,768,192]{1,2,0:T(8,128)(2,1)S(1)}, bf16[3,768,192]{1,2,0:T(8,128)(2,1)}, u32[]{:S(2)}) copy-start(bf16[3,768,192]{1,2,0:T(8,128)(2,1)} %param.8) | copy-start | bytes 2654212
  3.0 0.7 %copy-start.3 = (bf16[1,512,192]{1,2,0:T(8,128)(2,1)}, bf16[1,512,192]{1,2,0:T(8,128)(2,1)S(1)}, u32[]{:S(2)}) copy-start(bf16[1,512,192]{1,2,0:T(8,128)(2,1)S(1)} %get-tuple-element.21) | copy-start | bytes 589828
  3.0 1.0 %copy-start.1 = (bf16[1,512,192]{1,2,0:T(8,128)(2,1)}, bf16[1,512,192]{1,2,0:T(8,128)(2,1)S(1)}, u32[]{:S(2)}) copy-start(bf16[1,512,192]{1,2,0:T(8,128)(2,1)S(1)} %get-tuple-element.20) | copy-start | bytes 589828
  3.8 0.7 copy-start.10
  7.9 29.9 %collective-permute-start = (bf16[1,2,64,192]{3,2,1,0:T(8,128)(2,1)S(1)}, bf16[1,2,64,192]{3,2,1,0:T(8,128)(2,1)}, u32[]{:S(2)}, u32[]{:S(2)}) collective-permute-start(bf16[1,2,64,192]{3,2,1,0:T(8,128)(2,1)S(1)} %bitcast.121), channel_id=1, source_target_pairs={{0,4},{4,0},{8,12},{12,8},{1,5},{5,1},{9,13},{13,9},{2,6},{6,2},{1... | collective-permute-start | bytes 147464 | tf_op jit(solution)/shard_map/ppermute | solution.py:25
  12.9 45.1 %all-to-all-start = ((bf16[192,4,192]{0,2,1:T(8,128)(2,1)}), bf16[192,4,192]{0,2,1:T(8,128)(2,1)}, u32[]{:S(2)}, u32[]{:S(2)}) async-start(bf16[192,4,192]{0,2,1:T(8,128)(2,1)} %bitcast.24), calls=%async_computation | async-start | bytes 786432 | tf_op jit(solution)/shard_map/all_to_all | solution.py:141
  17.0 0.9 %copy-start.4 = (bf16[1,512,192]{1,2,0:T(8,128)(2,1)S(1)}, bf16[1,512,192]{1,2,0:T(8,128)(2,1)}, u32[]{:S(2)}) copy-start(bf16[1,512,192]{1,2,0:T(8,128)(2,1)} %copy-done.3) | copy-start | bytes 589828
  17.2 1.0 %copy-start.2 = (bf16[1,512,192]{1,2,0:T(8,128)(2,1)S(1)}, bf16[1,512,192]{1,2,0:T(8,128)(2,1)}, u32[]{:S(2)}) copy-start(bf16[1,512,192]{1,2,0:T(8,128)(2,1)} %copy-done.1) | copy-start | bytes 589828
  17.3 0.9 %copy-start.9 = (s32[3]{0:T(128)S(1)}, s32[3]{0:T(128)}, u32[]{:S(2)}) copy-start(s32[3]{0:T(128)} %param.13) | copy-start | bytes 40
  36.6 1.0 %copy-start.5 = (f32[4,128,3,64]{1,3,2,0:T(8,128)S(1)}, f32[4,128,3,64]{1,3,2,0:T(8,128)}, u32[]{:S(2)}) copy-start(f32[4,128,3,64]{1,3,2,0:T(8,128)} %fusion.1) | copy-start | bytes 1179652
  38.7 7.2 %collective-permute-start.1 = (bf16[2,2,64,192]{3,2,1,0:T(8,128)(2,1)S(1)}, bf16[2,2,64,192]{3,2,1,0:T(8,128)(2,1)S(1)}, u32[]{:S(2)}, u32[]{:S(2)}) collective-permute-start(bf16[2,2,64,192]{3,2,1,0:T(8,128)(2,1)S(1)} %pad_maximum_fusion), channel_id=1, source_target_pairs={{0,8},{4,12},{8,0},{12,4},{1,9},{5,13},{9,1},{13,5},{2,10},{6,14},... | collective-permute-start | bytes 294920 | tf_op jit(solution)/shard_map/ppermute | solution.py:25
  40.7 5.8 %copy-start.6 = (bf16[64,3,64]{2,1,0:T(4,128)(2,1)S(1)}, bf16[64,3,64]{2,1,0:T(4,128)(2,1)}, u32[]{:S(2)}) copy-start(bf16[64,3,64]{2,1,0:T(4,128)(2,1)} %get-tuple-element.10) | copy-start | bytes 73732
  59.3 6.8 %copy-start.7 = (f32[192]{0:T(256)S(1)}, f32[192]{0:T(256)}, u32[]{:S(2)}) copy-start(f32[192]{0:T(256)} %param.11) | copy-start | bytes 2308
  59.3 6.7 %copy-start.8 = (f32[192]{0:T(256)S(1)}, f32[192]{0:T(256)}, u32[]{:S(2)}) copy-start(f32[192]{0:T(256)} %param.10) | copy-start | bytes 2308
